TPU v7x, 32 devices: a whole 2x2x4 slice. The times are simulated.
32 devices in a mesh: grp: 8 (over z, x), seq: 4 (over y, core).
Axes of the slice: x: 2, y: 2, z: 4, core: 2. Of those that a mesh axis runs over, the one named last changes fastest.
Arguments:
- frames_in: bfloat16 [8192, 512], P(('grp', 'seq')), may hold values from -6 to 6
- norm_gain: float32 [512], replicated, may hold values from 0.25 to 1.75
- qkv_weight: bfloat16 [512, 1536], replicated, may hold values from -0.25 to 0.25
- conv_weight: float32 [4, 1536], replicated, may hold values from -3 to 3
- out_weight: bfloat16 [512, 512], replicated, may hold values from -0.25 to 0.25
- head_gain: float32 [512], replicated, may hold values from 0.25 to 1.75
- ffn_gain: float32 [512], replicated, may hold values from 0.25 to 1.75
- up_weight: bfloat16 [512, 2048], P(None, 'seq'), may hold values from -0.25 to 0.25
- down_weight: bfloat16 [2048, 512], P('seq'), may hold values from -0.125 to 0.125
Outputs:
- encoded: bfloat16 [8192, 512], P(('grp', 'seq'))
All inputs are finite; a program needn't handle non-finite values.
Results may differ from a plain program's by a relative error of at most 0.007.
Values may be sent and summed in bfloat16 or wider, within the bound.
No kernel may reach another device: no remote copies, remote signals or barrier semaphores. Data moves between devices by JAX's collectives and lax.ppermute only.
A program may use at most 256 MiB of HBM per device.

v0:
```python
import jax
import jax.numpy as jnp
from jax import lax
from jax.sharding import PartitionSpec as P

HEADS = 8
HEAD = 64
KERNEL = 4
BLOCK = 256
EPSILON = 1e-05


def from_behind(block, axis, distance):
    devices = range(lax.axis_size(axis))
    route = [(i - distance, i) for i in devices if i - distance in devices]
    return lax.ppermute(block, axis, route)


def prefix_2(x, axis, combine, identity):
    length, place = (lax.axis_size(axis), lax.axis_index(axis))
    everything = lax.all_gather(x, axis)
    start = jnp.broadcast_to(jnp.asarray(identity, x.dtype), x.shape)

    def turn(k, before):
        reached = k < place
        new = combine(before, everything[k])
        return jnp.where(reached, new, before)

    return lax.fori_loop(0, length, turn, start)


def rms_scale(values_in, gain):
    mean_square = jnp.mean(values_in * values_in, axis=-1, keepdims=True)
    return values_in * lax.rsqrt(mean_square + EPSILON) * gain


def add_states(earlier, later):
    return earlier + later


def attend_block(pieces):
    queries, key_rows, value_rows, state_low = pieces
    block_len = queries.shape[0]
    causal = jnp.arange(block_len)[:, None] >= jnp.arange(block_len)[None, :]
    scores = jnp.einsum("thd,shd->hts", queries, key_rows, preferred_element_type=jnp.float32)
    scores = jnp.where(causal[None], scores, 0.0).astype(jnp.bfloat16)
    local_part = jnp.einsum("hts,shd->thd", scores, value_rows, preferred_element_type=jnp.float32)
    carried_part = jnp.einsum(
        "thd,hde->the", queries, state_low, preferred_element_type=jnp.float32
    )
    return local_part + carried_part


def body(
    frames_in,
    norm_gain,
    qkv_weight,
    conv_weight,
    out_weight,
    head_gain,
    ffn_gain,
    up_weight,
    down_weight,
):
    row_count, model_width = frames_in.shape
    block_count = row_count // BLOCK
    lag_rows = KERNEL - 1
    normed = rms_scale(frames_in.astype(jnp.float32), norm_gain).astype(jnp.bfloat16)
    projected = jnp.dot(normed, qkv_weight, preferred_element_type=jnp.float32).astype(jnp.bfloat16)
    before = from_behind(projected[row_count - lag_rows :], ("grp", "seq"), 1)
    extended = jnp.concatenate([before, projected], axis=0).astype(jnp.float32)
    convolved = jnp.zeros((row_count, 3 * model_width), jnp.float32)
    for offset in range(KERNEL):
        convolved = (
            convolved
            + conv_weight[offset] * extended[lag_rows - offset : lag_rows - offset + row_count]
        )
    block_shape = (block_count, BLOCK, HEADS, HEAD)
    queries = jax.nn.silu(convolved[:, :model_width]).astype(jnp.bfloat16).reshape(block_shape)
    key_rows = (
        jax.nn.silu(convolved[:, model_width : 2 * model_width])
        .astype(jnp.bfloat16)
        .reshape(block_shape)
    )
    value_rows = convolved[:, 2 * model_width :].astype(jnp.bfloat16).reshape(block_shape)
    block_states = jnp.einsum(
        "bshd,bshe->bhde", key_rows, value_rows, preferred_element_type=jnp.float32
    )
    device_state = jnp.sum(block_states, axis=0)
    zero_state = jnp.zeros_like(device_state)
    prefix = prefix_2(device_state, ("grp", "seq"), add_states, zero_state)
    earlier_blocks = jnp.concatenate(
        [zero_state[None], jnp.cumsum(block_states[:-1], axis=0)], axis=0
    )
    state_low = (prefix[None] + earlier_blocks).astype(jnp.bfloat16)
    attended = lax.map(attend_block, (queries, key_rows, value_rows, state_low))
    head_square = jnp.mean(attended * attended, axis=-1, keepdims=True)
    headed = (attended * lax.rsqrt(head_square + EPSILON)).reshape(
        row_count, model_width
    ) * head_gain
    headed = headed.astype(jnp.bfloat16)
    residual = frames_in.astype(jnp.float32) + jnp.dot(
        headed, out_weight, preferred_element_type=jnp.float32
    )
    normed_ffn = rms_scale(residual, ffn_gain).astype(jnp.bfloat16)
    inner_act = jax.nn.gelu(
        jnp.dot(
            normed_ffn,
            lax.all_gather(up_weight, "seq", axis=1, tiled=True),
            preferred_element_type=jnp.float32,
        )
    ).astype(jnp.bfloat16)
    ffn_out = jnp.dot(
        inner_act,
        lax.all_gather(down_weight, "seq", axis=0, tiled=True),
        preferred_element_type=jnp.float32,
    )
    return (residual + ffn_out).astype(jnp.bfloat16)


def solution(mesh):
    in_specs = (
        P(("grp", "seq"), None),
        P(),
        P(),
        P(),
        P(),
        P(),
        P(),
        P(None, "seq"),
        P("seq", None),
    )
    out_specs = P(("grp", "seq"), None)
    return jax.shard_map(body, mesh=mesh, in_specs=in_specs, out_specs=out_specs, check_vma=False)
```

profile of v0, /device:TPU:0, one launch (start us, length us, event | category | flops | bytes accessed | tf_op | source)
XLA Modules:
  0.0 155.0 jit_solution(5738290194023966455)
XLA Ops:
  6.5 1.2 fusion.21
  8.0 1.6 %convolution_convert_fusion = bf16[256,1536]{1,0:T(8,128)(2,1)S(1)} fusion(bf16[512,1536]{1,0:T(8,128)(2,1)S(1)} %copy-done, bf16[256,512]{1,0:T(8,128)(2,1)} %param.11, f32[512]{0:T(512)} %param.12, f32[256]{0:T(256)S(1)} %add_rsqrt_fusion.2), kind=kOutput, calls=%fused_computation.2 | convolution fusion | flops 403570688 | bytes 2624512 | tf_op jit(solution)/shard_map/dot_general | solution.py:69
  9.6 2.4 %collective-permute-start = (bf16[3,1536]{1,0:T(4,128)(2,1)S(1)}, bf16[3,1536]{1,0:T(4,128)(2,1)S(1)}, u32[]{:S(2)}, u32[]{:S(2)}) collective-permute-start(bf16[3,1536]{1,0:T(4,128)(2,1)S(1)} %slice.49), channel_id=1, source_target_pairs={{0,1},{1,2},{2,3},{3,4},{4,5},{5,6},{6,7},{7,8},{8,9},{9,10},{10,1... | collective-permute-start | bytes 27656 | tf_op jit(solution)/shard_map/ppermute | solution.py:16
  17.0 80.1 %all-gather.9.cloned.1.call-done = f32[256,64,64]{2,1,0:T(8,128)} async-done(((f32[8,64,64]{2,1,0:T(8,128)}), f32[256,64,64]{2,1,0:T(8,128)}) %all-gather.9.cloned.1.call-update) | async-done | bytes 4194320 | tf_op jit(solution)/shard_map/all_gather | solution.py:21
  97.0 34.4 %while.18 = (s32[]{:T(128)}, f32[8,64,64]{2,1,0:T(8,128)S(1)}, s32[]{:T(128)}, f32[32,8,64,64]{3,2,1,0:T(8,128)}, s32[]{:T(128)}, /*index=5*/s32[]{:T(128)}) while((s32[]{:T(128)}, f32[8,64,64]{2,1,0:T(8,128)S(1)}, s32[]{:T(128)}, f32[32,8,64,64]{3,2,1,0:T(8,128)}, s32[]{:T(128)}, /*index=5*/s32[]{:T(128)}) %tuple.49), condition=%wide.region_2.3_spmd.clone, body=%wide.region_1.2_spmd.clone.sunk | while | flops 98308 | bytes 393309 | solution.py:29
  98.1 1.0 add_select_fusion.2
  99.2 1.0 add_select_fusion.2
  100.2 1.0 add_select_fusion.2
  101.3 1.0 add_select_fusion.2
  102.4 1.1 add_select_fusion.2
  103.5 1.1 add_select_fusion.2
  104.6 1.1 add_select_fusion.2
  105.7 1.0 add_select_fusion.2
  106.8 1.0 add_select_fusion.2
  107.9 1.0 add_select_fusion.2
  108.9 1.0 add_select_fusion.2
  110.0 1.0 add_select_fusion.2
  111.1 1.0 add_select_fusion.2
  112.1 1.0 add_select_fusion.2
  113.2 1.0 add_select_fusion.2
  114.3 1.0 add_select_fusion.2
  115.3 1.0 add_select_fusion.2
  116.4 1.0 add_select_fusion.2
  117.5 1.0 add_select_fusion.2
  127.1 1.1 add_select_fusion.2
  128.2 1.1 add_select_fusion.2
  129.3 1.1 add_select_fusion.2
  131.5 1.1 fusion.33
  132.5 1.8 %multiply_reduce_fusion.1 = (f32[256,8]{0,1:T(8,128)S(1)}, f32[256,8,64]{0,2,1:T(8,128)S(1)}) fusion(f32[8,64,256]{2,1,0:T(8,128)} %fusion.33, bf16[256,8,64]{0,2,1:T(8,128)(2,1)S(1)} %bitcast.28, bf16[256,8,64]{0,2,1:T(8,128)(2,1)S(1)} %bitcast.30, bf16[256,8,64]{0,2,1:T(8,128)(2,1)S(1)} %bitcast.26, pred[256,256]{1,0:T(8,128)(4,1)S(1)} %iota_compare_fusion), kind=kOutput, calls=%fused_computation.41 | convolution fusion | flops 135657472 | bytes 1908736 | tf_op jit(solution)/shard_map/while/body/eval_jaxpr/hts,shd->thd/dot_general | solution.py:47
  134.6 1.5 multiply_reduce_fusion
  136.1 7.9 %all-gather.7.cloned.1.call-done = bf16[2048,512]{1,0:T(8,128)(2,1)} async-done(((bf16[512,512]{1,0:T(8,128)(2,1)}), bf16[2048,512]{1,0:T(8,128)(2,1)}) %all-gather.7.cloned.1.call-update) | async-done | bytes 2097168 | tf_op jit(solution)/shard_map/all_gather | solution.py:115
  144.0 4.5 %fusion.14 = bf16[256,512]{1,0:T(8,128)(2,1)} fusion(f32[256,512]{1,0:T(8,128)S(1)} %get-tuple-element.135, bf16[2048,512]{1,0:T(8,128)(2,1)} %all-gather.7.cloned.1.call-done, bf16[512,2048]{1,0:T(8,128)(2,1)} %all-gather.5.cloned.1.call-done, f32[512]{0:T(512)S(1)} %copy-done.4, f32[256]{0:T(256)S(1)} %add_rsqrt_fusion.1), kind=kOutput, calls=%fused_computation.24 | convolution fusion | flops 1079115776 | bytes 4983808 | tf_op jit(solution)/shard_map/dot_general | solution.py:113
  (45 shorter events, 15.8 us)
Async XLA Ops:
  6.5 1.5 copy-start
  6.5 5.5 %copy-start.2 = (f32[4,1536]{1,0:T(4,128)S(1)}, f32[4,1536]{1,0:T(4,128)}, u32[]{:S(2)}) copy-start(f32[4,1536]{1,0:T(4,128)} %param.14) | copy-start | bytes 73732
  6.5 90.5 %all-gather.9.cloned.1.call-start = ((), (), s32[]{:S(2)}) async-start(), calls=%async_computation.2 | async-start | bytes 8650752 | tf_op jit(solution)/shard_map/all_gather | solution.py:21
  9.6 3.2 %collective-permute-start = (bf16[3,1536]{1,0:T(4,128)(2,1)S(1)}, bf16[3,1536]{1,0:T(4,128)(2,1)S(1)}, u32[]{:S(2)}, u32[]{:S(2)}) collective-permute-start(bf16[3,1536]{1,0:T(4,128)(2,1)S(1)} %slice.49), channel_id=1, source_target_pairs={{0,1},{1,2},{2,3},{3,4},{4,5},{5,6},{6,7},{7,8},{8,9},{9,10},{10,1... | collective-permute-start | bytes 27656 | tf_op jit(solution)/shard_map/ppermute | solution.py:16
  15.3 120.8 %all-gather.5.cloned.1.call-start = ((), (), s32[]{:S(2)}) async-start(), calls=%async_computation | async-start | bytes 2621440 | tf_op jit(solution)/shard_map/all_gather | solution.py:109
  16.0 127.9 %all-gather.7.cloned.1.call-start = ((), (), s32[]{:S(2)}) async-start(), calls=%async_computation.1 | async-start | bytes 2621440 | tf_op jit(solution)/shard_map/all_gather | solution.py:115
  131.4 3.0 %copy-start.3 = (f32[512]{0:T(512)S(1)}, f32[512]{0:T(512)}, u32[]{:S(2)}) copy-start(f32[512]{0:T(512)} %param.16) | copy-start | bytes 6148
  132.5 2.1 %copy-start.1 = (bf16[256,512]{1,0:T(8,128)(2,1)S(1)}, bf16[256,512]{1,0:T(8,128)(2,1)}, u32[]{:S(2)}) copy-start(bf16[256,512]{1,0:T(8,128)(2,1)} %param.11) | copy-start | bytes 786436
  134.4 9.6 %copy-start.4 = (f32[512]{0:T(512)S(1)}, f32[512]{0:T(512)}, u32[]{:S(2)}) copy-start(f32[512]{0:T(512)} %param.17) | copy-start | bytes 6148
Sparse Core Ops, SparseCore 0:
  15.4 81.5 all-gather.8
  98.6 21.1 all-gather.4
  121.4 22.5 all-gather.6
where the time goes:
time: 156 us; the launch traced here: 155 us
  waiting for transfers between devices  90.1 us (58%)
  other arithmetic  36.2 us (23%)
  between operations  13.3 us (9%)
  matrix products  11.4 us (7%)
  starting transfers between devices  2.48 us (2%)
    all_gather x1, waiting for transfers between devices, prefix_2(): everything = lax.all_gather(x, axis)  80.1 us
    select_n x32, other arithmetic, turn(): return jnp.where(reached, new, before)  33.6 us
    all_gather x1, waiting for transfers between devices, body(): lax.all_gather(down_weight, 'seq', axis=0, tiled=True)  7.88 us
    dot_general x1, matrix products, body(): jnp.dot(inner_act, lax.all_gather(down_weight, 'seq', axis=0, tiled=True)...  4.54 us
  transfers between devices with their start and end apart: 4, of which 3 were waited for; matrix products, arithmetic and copies ran while one was open for 25% of the time, Pallas kernels for 0%

commit v1 on v0

--- a/solution.py
+++ b/solution.py
@@ -8,6 +8,16 @@
 KERNEL = 4
 BLOCK = 256
 EPSILON = 1e-05
+
+
+def collect(x, axis, dim):
+    ways, here, step = (lax.axis_size(axis), lax.axis_index(axis), x.shape[dim])
+    dims = [n * ways if d == dim else n for d, n in enumerate(x.shape)]
+    full = lax.dynamic_update_slice_in_dim(jnp.zeros(dims, x.dtype), x, here * step, axis=dim)
+    for far in range(1, ways):
+        x = lax.ppermute(x, axis, [(d, (d + 1) % ways) for d in range(ways)])
+        full = lax.dynamic_update_slice_in_dim(full, x, (here - far) % ways * step, axis=dim)
+    return full
 
 
 def from_behind(block, axis, distance):
@@ -110,11 +120,7 @@
             preferred_element_type=jnp.float32,
         )
     ).astype(jnp.bfloat16)
-    ffn_out = jnp.dot(
-        inner_act,
-        lax.all_gather(down_weight, "seq", axis=0, tiled=True),
-        preferred_element_type=jnp.float32,
-    )
+    ffn_out = jnp.dot(inner_act, collect(down_weight, "seq", 0), preferred_element_type=jnp.float32)
     return (residual + ffn_out).astype(jnp.bfloat16)
 
 

time: 156 us -> 149 us (0.955)
  waiting for transfers between devices: 90.1 us -> 70.5 us
  local copies, waits for them, and re-layouts: 0.8 us -> 9.51 us
  starting transfers between devices: 2.48 us -> 5.62 us
    all_gather x1, waiting for transfers between devices: 80.1 us -> 49.1 us  [prefix_2(): everything = lax.all_gather(x, axis)]
    ppermute x0 -> x3, waiting for transfers between devices: none -> 20.6 us  [collect(): x = lax.ppermute(x, axis, [(d, (d + 1) % ways) for d in range(ways)])]
    all_gather x1 -> x0, waiting for transfers between devices: 7.88 us -> none  [body(): lax.all_gather(down_weight, 'seq', axis=0, tiled=True)]
    dynamic_update_slice x0 -> x4, local copies, waits for them, and re-layouts: none -> 6.48 us  [the longest x3 5.63 us: collect(): lax.dynamic_update_slice_in_dim(full, x, (here - far) % ways * step, axis...]
    ppermute x0 -> x3, starting transfers between devices: none -> 3.18 us  [collect(): x = lax.ppermute(x, axis, [(d, (d + 1) % ways) for d in range(ways)])]
  transfers between devices with their start and end apart: 4 -> 6, of which waited for: 3 -> 5; matrix products, arithmetic and copies ran while one was open for 25% -> 31% of each run, Pallas kernels for 0% -> 0%
where the time goes in v1:
time: 149 us; the launch traced here: 148 us
  waiting for transfers between devices  70.5 us (47%)
  other arithmetic  36.2 us (24%)
  between operations  13.7 us (9%)
  matrix products  11.4 us (8%)
  local copies, waits for them, and re-layouts  9.51 us (6%)
  starting transfers between devices  5.62 us (4%)
    all_gather x1, waiting for transfers between devices, prefix_2(): everything = lax.all_gather(x, axis)  49.1 us
    select_n x32, other arithmetic, turn(): return jnp.where(reached, new, before)  33.6 us
    ppermute x3, waiting for transfers between devices, collect(): x = lax.ppermute(x, axis, [(d, (d + 1) % ways) for d in range(ways)])  20.6 us
    dynamic_update_slice x3, local copies, waits for them, and re-layouts, collect(): lax.dynamic_update_slice_in_dim(full, x, (here - far) % ways * step, axis...  5.63 us
    dot_general x1, matrix products, body(): jnp.dot(inner_act, collect(down_weight, 'seq', 0), preferred_element_type...  4.54 us
    ppermute x3, starting transfers between devices, collect(): x = lax.ppermute(x, axis, [(d, (d + 1) % ways) for d in range(ways)])  3.18 us
  transfers between devices with their start and end apart: 6, of which 5 were waited for; matrix products, arithmetic and copies ran while one was open for 31% of the time, Pallas kernels for 0%

profile of v1, /device:TPU:0, one launch (start us, length us, event | category | flops | bytes accessed | tf_op | source)
XLA Modules:
  0.0 147.7 jit_solution(13361155009467363885)
XLA Ops:
  6.5 1.2 fusion.21
  8.0 1.6 %convolution_convert_fusion = bf16[256,1536]{1,0:T(8,128)(2,1)S(1)} fusion(bf16[512,1536]{1,0:T(8,128)(2,1)S(1)} %copy-done, bf16[256,512]{1,0:T(8,128)(2,1)} %param.11, f32[512]{0:T(512)} %param.12, f32[256]{0:T(256)S(1)} %add_rsqrt_fusion.2), kind=kOutput, calls=%fused_computation.2 | convolution fusion | flops 403570688 | bytes 2624512 | tf_op jit(solution)/shard_map/dot_general | solution.py:79
  9.6 2.4 %collective-permute-start = (bf16[3,1536]{1,0:T(4,128)(2,1)S(1)}, bf16[3,1536]{1,0:T(4,128)(2,1)S(1)}, u32[]{:S(2)}, u32[]{:S(2)}) collective-permute-start(bf16[3,1536]{1,0:T(4,128)(2,1)S(1)} %slice.49), channel_id=1, source_target_pairs={{0,1},{1,2},{2,3},{3,4},{4,5},{5,6},{6,7},{7,8},{8,9},{9,10},{10,1... | collective-permute-start | bytes 27656 | tf_op jit(solution)/shard_map/ppermute | solution.py:26
  15.4 2.7 %collective-permute-start.1 = (bf16[512,512]{1,0:T(8,128)(2,1)S(1)}, bf16[512,512]{1,0:T(8,128)(2,1)S(1)}, u32[]{:S(2)}, u32[]{:S(2)}) collective-permute-start(bf16[512,512]{1,0:T(8,128)(2,1)S(1)} %copy-done.2), channel_id=1, source_target_pairs={{0,1},{1,2},{2,3},{3,0},{4,5},{5,6},{6,7},{7,4},{8,9},{9,10},{10,1... | collective-permute-start | bytes 1572872 | tf_op jit(solution)/shard_map/ppermute | solution.py:18
  18.0 7.9 %collective-permute-done.1 = bf16[512,512]{1,0:T(8,128)(2,1)S(1)} collective-permute-done((bf16[512,512]{1,0:T(8,128)(2,1)S(1)}, bf16[512,512]{1,0:T(8,128)(2,1)S(1)}, u32[]{:S(2)}, u32[]{:S(2)}) %collective-permute-start.1) | collective-permute-done | bytes 524320 | tf_op jit(solution)/shard_map/ppermute | solution.py:18
  27.2 10.1 %collective-permute-done.2 = bf16[512,512]{1,0:T(8,128)(2,1)} collective-permute-done((bf16[512,512]{1,0:T(8,128)(2,1)S(1)}, bf16[512,512]{1,0:T(8,128)(2,1)}, u32[]{:S(2)}, u32[]{:S(2)}) %collective-permute-start.2) | collective-permute-done | bytes 524320 | tf_op jit(solution)/shard_map/ppermute | solution.py:18
  37.4 1.4 broadcast_in_dim.42
  39.9 1.9 %constant_dynamic-update-slice_fusion.2 = bf16[2048,512]{1,0:T(8,128)(2,1)} fusion(bf16[2048,512]{1,0:T(8,128)(2,1)} %constant_dynamic-update-slice_fusion.3, bf16[512,512]{1,0:T(8,128)(2,1)} %copy-done.3, s32[]{:T(128)S(6)} %select_n.56), kind=kLoop, calls=%fused_computation.61 | loop fusion | bytes 1048580 | tf_op jit(solution)/shard_map/dynamic_update_slice | solution.py:19
  41.8 1.9 %constant_dynamic-update-slice_fusion.1 = bf16[2048,512]{1,0:T(8,128)(2,1)} fusion(bf16[2048,512]{1,0:T(8,128)(2,1)} %constant_dynamic-update-slice_fusion.2, bf16[512,512]{1,0:T(8,128)(2,1)} %collective-permute-done.2, s32[]{:T(128)S(6)} %select_n.58), kind=kLoop, calls=%fused_computation.60 | loop fusion | bytes 1048580 | tf_op jit(solution)/shard_map/dynamic_update_slice | solution.py:19
  43.6 2.6 %collective-permute-done.3 = bf16[512,512]{1,0:T(8,128)(2,1)} collective-permute-done((bf16[512,512]{1,0:T(8,128)(2,1)}, bf16[512,512]{1,0:T(8,128)(2,1)}, u32[]{:S(2)}, u32[]{:S(2)}) %collective-permute-start.3) | collective-permute-done | bytes 524320 | tf_op jit(solution)/shard_map/ppermute | solution.py:18
  46.2 1.9 %constant_dynamic-update-slice_fusion = bf16[2048,512]{1,0:T(8,128)(2,1)} fusion(bf16[2048,512]{1,0:T(8,128)(2,1)} %constant_dynamic-update-slice_fusion.1, bf16[512,512]{1,0:T(8,128)(2,1)} %collective-permute-done.3, s32[]{:T(128)S(6)} %select_n.60), kind=kLoop, calls=%fused_computation.59 | loop fusion | bytes 1048580 | tf_op jit(solution)/shard_map/dynamic_update_slice | solution.py:19
  48.1 49.1 %all-gather.6.cloned.1.call-done = f32[256,64,64]{2,1,0:T(8,128)} async-done(((f32[8,64,64]{2,1,0:T(8,128)}), f32[256,64,64]{2,1,0:T(8,128)}) %all-gather.6.cloned.1.call-update) | async-done | bytes 4194320 | tf_op jit(solution)/shard_map/all_gather | solution.py:31
  97.2 34.4 %while.18 = (s32[]{:T(128)}, f32[8,64,64]{2,1,0:T(8,128)S(1)}, s32[]{:T(128)}, f32[32,8,64,64]{3,2,1,0:T(8,128)}, s32[]{:T(128)}, /*index=5*/s32[]{:T(128)}) while((s32[]{:T(128)}, f32[8,64,64]{2,1,0:T(8,128)S(1)}, s32[]{:T(128)}, f32[32,8,64,64]{3,2,1,0:T(8,128)}, s32[]{:T(128)}, /*index=5*/s32[]{:T(128)}) %tuple.47), condition=%wide.region_2.3_spmd.clone, body=%wide.region_1.2_spmd.clone.sunk | while | flops 98308 | bytes 393317 | solution.py:39
  98.3 1.0 add_select_fusion.2
  99.4 1.0 add_select_fusion.2
  100.4 1.0 add_select_fusion.2
  101.5 1.0 add_select_fusion.2
  102.6 1.1 add_select_fusion.2
  103.7 1.1 add_select_fusion.2
  104.8 1.1 add_select_fusion.2
  105.9 1.0 add_select_fusion.2
  107.0 1.0 add_select_fusion.2
  108.1 1.0 add_select_fusion.2
  109.1 1.0 add_select_fusion.2
  110.2 1.0 add_select_fusion.2
  111.3 1.0 add_select_fusion.2
  118.8 1.0 add_select_fusion.2
  119.8 1.0 add_select_fusion.2
  131.6 1.1 fusion.33
  132.7 1.8 %multiply_reduce_fusion.1 = (f32[256,8]{0,1:T(8,128)S(1)}, f32[256,8,64]{0,2,1:T(8,128)S(1)}) fusion(f32[8,64,256]{2,1,0:T(8,128)} %fusion.33, bf16[256,8,64]{0,2,1:T(8,128)(2,1)S(1)} %bitcast.28, bf16[256,8,64]{0,2,1:T(8,128)(2,1)S(1)} %bitcast.30, bf16[256,8,64]{0,2,1:T(8,128)(2,1)S(1)} %bitcast.26, pred[256,256]{1,0:T(8,128)(4,1)S(1)} %iota_compare_fusion), kind=kOutput, calls=%fused_computation.41 | convolution fusion | flops 135657472 | bytes 1908736 | tf_op jit(solution)/shard_map/while/body/eval_jaxpr/hts,shd->thd/dot_general | solution.py:57
  134.8 1.4 multiply_reduce_fusion
  136.3 4.5 %fusion.14 = bf16[256,512]{1,0:T(8,128)(2,1)} fusion(f32[256,512]{1,0:T(8,128)S(1)} %get-tuple-element.135, bf16[2048,512]{1,0:T(8,128)(2,1)} %constant_dynamic-update-slice_fusion, bf16[512,2048]{1,0:T(8,128)(2,1)} %all-gather.4.cloned.1.call-done, f32[512]{0:T(512)S(1)} %copy-done.6, f32[256]{0:T(256)S(1)} %add_rsqrt_fusion.1), kind=kOutput, calls=%fused_computation.24 | convolution fusion | flops 1079115776 | bytes 4983808 | tf_op jit(solution)/shard_map/dot_general | solution.py:123
  (57 shorter events, 23.9 us)
Async XLA Ops:
  6.5 1.5 %copy-start = (bf16[512,1536]{1,0:T(8,128)(2,1)S(1)}, bf16[512,1536]{1,0:T(8,128)(2,1)}, u32[]{:S(2)}) copy-start(bf16[512,1536]{1,0:T(8,128)(2,1)} %param.13) | copy-start | bytes 4718596
  6.5 5.5 %copy-start.4 = (f32[4,1536]{1,0:T(4,128)S(1)}, f32[4,1536]{1,0:T(4,128)}, u32[]{:S(2)}) copy-start(f32[4,1536]{1,0:T(4,128)} %param.14) | copy-start | bytes 73732
  6.5 90.7 %all-gather.6.cloned.1.call-start = ((), (), s32[]{:S(2)}) async-start(), calls=%async_computation.1 | async-start | bytes 8650752 | tf_op jit(solution)/shard_map/all_gather | solution.py:31
  9.6 3.2 %collective-permute-start = (bf16[3,1536]{1,0:T(4,128)(2,1)S(1)}, bf16[3,1536]{1,0:T(4,128)(2,1)S(1)}, u32[]{:S(2)}, u32[]{:S(2)}) collective-permute-start(bf16[3,1536]{1,0:T(4,128)(2,1)S(1)} %slice.49), channel_id=1, source_target_pairs={{0,1},{1,2},{2,3},{3,4},{4,5},{5,6},{6,7},{7,8},{8,9},{9,10},{10,1... | collective-permute-start | bytes 27656 | tf_op jit(solution)/shard_map/ppermute | solution.py:26
  13.7 1.6 %copy-start.2 = (bf16[512,512]{1,0:T(8,128)(2,1)S(1)}, bf16[512,512]{1,0:T(8,128)(2,1)}, u32[]{:S(2)}) copy-start(bf16[512,512]{1,0:T(8,128)(2,1)} %param.19) | copy-start | bytes 1572868
  15.3 120.9 %all-gather.4.cloned.1.call-start = ((), (), s32[]{:S(2)}) async-start(), calls=%async_computation | async-start | bytes 2621440 | tf_op jit(solution)/shard_map/all_gather | solution.py:119
  15.4 10.6 %collective-permute-start.1 = (bf16[512,512]{1,0:T(8,128)(2,1)S(1)}, bf16[512,512]{1,0:T(8,128)(2,1)S(1)}, u32[]{:S(2)}, u32[]{:S(2)}) collective-permute-start(bf16[512,512]{1,0:T(8,128)(2,1)S(1)} %copy-done.2), channel_id=1, source_target_pairs={{0,1},{1,2},{2,3},{3,0},{4,5},{5,6},{6,7},{7,4},{8,9},{9,10},{10,1... | collective-permute-start | bytes 1572872 | tf_op jit(solution)/shard_map/ppermute | solution.py:18
  25.9 0.8 copy-start.3
  26.7 10.6 %collective-permute-start.2 = (bf16[512,512]{1,0:T(8,128)(2,1)S(1)}, bf16[512,512]{1,0:T(8,128)(2,1)}, u32[]{:S(2)}, u32[]{:S(2)}) collective-permute-start(bf16[512,512]{1,0:T(8,128)(2,1)S(1)} %collective-permute-done.1), channel_id=1, source_target_pairs={{0,1},{1,2},{2,3},{3,0},{4,5},{5,6},{6,7},{7,4},{8,9},{9,10},{10,1... | collective-permute-start | bytes 1572872 | tf_op jit(solution)/shard_map/ppermute | solution.py:18
  37.3 8.9 %collective-permute-start.3 = (bf16[512,512]{1,0:T(8,128)(2,1)}, bf16[512,512]{1,0:T(8,128)(2,1)}, u32[]{:S(2)}, u32[]{:S(2)}) collective-permute-start(bf16[512,512]{1,0:T(8,128)(2,1)} %collective-permute-done.2), channel_id=1, source_target_pairs={{0,1},{1,2},{2,3},{3,0},{4,5},{5,6},{6,7},{7,4},{8,9},{9,10},{10,1... | collective-permute-start | bytes 1572872 | tf_op jit(solution)/shard_map/ppermute | solution.py:18
  131.6 3.0 %copy-start.5 = (f32[512]{0:T(512)S(1)}, f32[512]{0:T(512)}, u32[]{:S(2)}) copy-start(f32[512]{0:T(512)} %param.16) | copy-start | bytes 6148
  132.7 2.1 %copy-start.1 = (bf16[256,512]{1,0:T(8,128)(2,1)S(1)}, bf16[256,512]{1,0:T(8,128)(2,1)}, u32[]{:S(2)}) copy-start(bf16[256,512]{1,0:T(8,128)(2,1)} %param.11) | copy-start | bytes 786436
  134.5 1.7 %copy-start.6 = (f32[512]{0:T(512)S(1)}, f32[512]{0:T(512)}, u32[]{:S(2)}) copy-start(f32[512]{0:T(512)} %param.17) | copy-start | bytes 6148
Sparse Core Ops, SparseCore 0:
  15.4 81.7 all-gather.5
  98.8 21.1 all-gather.3
